TPU v7x, 32 devices: a whole 2x2x4 slice. The times are simulated.
32 devices in a mesh: grp: 4 (over z), inner: 8 (over y, x, core).
Axes of the slice: x: 2, y: 2, z: 4, core: 2. Of those that a mesh axis runs over, the one named last changes fastest.
Arguments:
- design: float32 [8, 4096, 1024], P('inner', 'grp'), may hold values from -6 to 6
- row_signs: int32 [8, 4096], P('inner', 'grp'), may hold values from 0 to 1
- kept_rows: int32 [8, 2048], P('inner'), may hold values from 0 to 4095, as said below
Outputs:
- factored: float32 [2048, 1024], P('grp')
Inputs may be any that keep to these rules, and one draw needn't show every extreme that they name: `kept_rows`: within each block the 2048 kept row numbers are distinct, and each block keeps its first and its last row.
All inputs are finite; a program needn't handle non-finite values.
Results may differ from a plain program's by a relative error of at most 0.0048.
Values may be sent and summed in bfloat16 or wider, within the bound.
No kernel may reach another device: no remote copies, remote signals or barrier semaphores. Data moves between devices by JAX's collectives and lax.ppermute only.
A program may use at most 64 MiB of HBM per device.

v0:
```python
import math
import jax
import jax.numpy as jnp
from jax import lax
from jax.sharding import PartitionSpec as P

COLS_DONE = 8
epsilon = 1e-06


def sign_table(row_ids, col_ids):
    common_bits = jnp.bitwise_and(row_ids[:, None], col_ids[None, :])
    ones_total = jnp.zeros(common_bits.shape, jnp.int32)
    for bit_pos in range(4):
        ones_total = ones_total + jnp.bitwise_and(jnp.right_shift(common_bits, bit_pos), 1)
    return 1.0 - 2.0 * jnp.bitwise_and(ones_total, 1).astype(jnp.float32)


def pick_rows(table_rows, chosen_rows):
    return jnp.take(table_rows, chosen_rows, axis=0)


def on_device(design, row_signs, kept_rows):
    block_count, local_rows, columns = design.shape
    keep_count = kept_rows.shape[1]
    groups = lax.axis_size("grp")
    owned_rows = keep_count // groups
    highest = lax.Precision.HIGHEST
    sixteen = jnp.arange(16, dtype=jnp.int32)
    hadamard = sign_table(sixteen, sixteen).astype(jnp.bfloat16)
    flipped = (design * (1 - 2 * row_signs).astype(jnp.float32)[:, :, None]).astype(jnp.bfloat16)
    lowest = flipped.reshape(block_count * local_rows // 16, 16, columns)
    first_pass = jnp.einsum(
        "hc,ncd->nhd", hadamard, lowest, preferred_element_type=jnp.float32
    ).astype(jnp.bfloat16)
    middle_view = first_pass.reshape(block_count * local_rows // 256, 16, 16, columns)
    second_pass = jnp.einsum(
        "hb,mbcd->mhcd", hadamard, middle_view, preferred_element_type=jnp.float32
    ).astype(jnp.bfloat16)
    second_pass = second_pass.reshape(block_count, local_rows, columns)
    gathered_rows = lax.all_to_all(second_pass, "grp", split_axis=2, concat_axis=1, tiled=True)
    col_count = gathered_rows.shape[2]
    by_piece = gathered_rows.reshape(block_count, 16, 256, col_count)
    mixed_rows = jnp.einsum("ha,nakd->nhkd", hadamard, by_piece, preferred_element_type=jnp.float32)
    mixed_rows = mixed_rows.reshape(block_count, 16 * 256, col_count)
    picked = jax.vmap(pick_rows)(mixed_rows, kept_rows)
    partial_value = jnp.sum(picked, axis=0)
    summed = lax.psum(partial_value, "inner")
    sketch = lax.all_to_all(summed, "grp", split_axis=0, concat_axis=1, tiled=True)
    sketch = sketch * (1.0 / (64.0 * math.sqrt(keep_count)))
    row_base = lax.axis_index("grp") * owned_rows
    global_rows = row_base + jnp.arange(owned_rows, dtype=jnp.int32)

    def reflect(col_index, current):
        column = jnp.where(global_rows >= col_index, current[:, col_index], 0.0)
        is_pivot = (global_rows == col_index).astype(jnp.float32)
        norm_sq, crossed, pivot_row = lax.psum(
            (
                jnp.sum(column * column),
                jnp.dot(column, current, precision=highest),
                jnp.dot(is_pivot, current, precision=highest),
            ),
            "grp",
        )
        pivot_value = pivot_row[col_index]
        head_value = -jnp.where(pivot_value >= 0, 1.0, -1.0) * jnp.sqrt(norm_sq)
        length = 2.0 * (norm_sq - head_value * pivot_value) + epsilon
        projected_row = crossed - head_value * pivot_row
        vector = column - head_value * is_pivot
        return current - vector[:, None] * (2.0 * projected_row / length)[None, :]

    result = lax.fori_loop(0, COLS_DONE, reflect, sketch)
    return result


def solution(mesh):
    return jax.shard_map(
        on_device,
        mesh=mesh,
        in_specs=(P("inner", "grp", None), P("inner", "grp"), P("inner", None)),
        out_specs=P("grp", None),
        check_vma=False,
    )
```

profile of v0, /device:TPU:0, one launch (start us, length us, event | category | flops | bytes accessed | tf_op | source)
XLA Modules:
  0.0 397.2 jit_solution(10092679646443896874)
XLA Ops:
  6.5 0.7 subtract_convert_fusion.4
  7.2 2.5 multiply_convert_fusion
  9.7 0.7 convolution_convert_fusion
  10.4 1.5 convert_bitcast_fusion
  11.9 1.2 copy.21
  13.1 7.7 %copy.22 = bf16[1,1024,1024]{1,0,2:T(2,128)(2,1)} copy(bf16[1,1024,1024]{2,1,0:T(8,128)(2,1)S(1)} %bitcast.77) | data formatting | bytes 4194304 | tf_op jit(solution)/shard_map/reshape | solution.py:40
  21.4 12.8 %reduce.2 = bf16[1024,1024]{1,0:T(8,128)(2,1)S(1)} reduce(bf16[1024,1,1024]{2,1,0:T(2,128)(2,1)} %bitcast.75, bf16[]{:T(256)} %broadcast.106), dimensions={1}, to_apply=%bitcast.43.reduce_sub_computation | reduce | bytes 4194306
  34.2 2.8 reshape.93
  36.9 6.5 %all-to-all-start = ((bf16[4,2,131072]{2,1,0:T(2,128)(2,1)}), bf16[4,2,131072]{2,1,0:T(2,128)(2,1)S(1)}, u32[]{:S(2)}, u32[]{:S(2)}) async-start(bf16[4,2,131072]{2,1,0:T(2,128)(2,1)} %reshape.93), calls=%async_computation | async-start | bytes 4194304 | tf_op jit(solution)/shard_map/all_to_all | solution.py:41
  43.5 48.1 %all-to-all-done = bf16[4,2,131072]{2,1,0:T(2,128)(2,1)S(1)} async-done(((bf16[4,2,131072]{2,1,0:T(2,128)(2,1)}), bf16[4,2,131072]{2,1,0:T(2,128)(2,1)S(1)}, u32[]{:S(2)}, u32[]{:S(2)}) %all-to-all-start) | async-done | bytes 2097184 | tf_op jit(solution)/shard_map/all_to_all | solution.py:41
  91.6 3.4 reshape.94
  94.9 3.0 copy.29
  97.9 2.6 copy.23
  100.5 2.9 convolution_bitcast_fusion
  103.4 4.4 %copy.25 = f32[1,16,256,256]{3,2,1,0:T(8,128)} copy(f32[1,16,256,256]{3,1,2,0:T(8,128)S(1)} %convolution_bitcast_fusion) | data formatting | bytes 8388608 | tf_op jit(solution)/shard_map/ha,nakd->nhkd/transpose | solution.py:44
  107.8 21.4 %gather_fusion = f32[2048,256]{1,0:T(8,128)S(1)} fusion(f32[1,4096,256]{2,1,0:T(8,128)} %bitcast.74, s32[2048]{0:T(1024)S(1)} %bitcast.73), kind=kCustom, calls=%fused_computation | custom fusion | bytes 4210688 | tf_op jit(solution)/shard_map/vmap(jit(_take))/gather | solution.py:20
  129.2 1.7 broadcast_select_fusion.2
  130.8 61.1 %all-reduce.5.cloned.1.call-done = f32[4,512,256]{2,1,0:T(8,128)} async-done(((f32[4,512,256]{2,1,0:T(8,128)}), f32[4,512,256]{2,1,0:T(8,128)}) %all-reduce.5.cloned.1.call-update) | async-done | bytes 2097168 | tf_op jit(solution)/shard_map/psum | solution.py:48
  191.9 4.5 %all-to-all-start.1 = ((f32[4,512,256]{2,1,0:T(8,128)}), f32[4,512,256]{2,1,0:T(8,128)S(1)}, u32[]{:S(2)}, u32[]{:S(2)}) async-start(f32[4,512,256]{2,1,0:T(8,128)} %all-reduce.5.cloned.1.call-done), calls=%async_computation.1 | async-start | bytes 4194304 | tf_op jit(solution)/shard_map/all_to_all | solution.py:49
  196.4 47.1 %all-to-all-done.1 = f32[4,512,256]{2,1,0:T(8,128)S(1)} async-done(((f32[4,512,256]{2,1,0:T(8,128)}), f32[4,512,256]{2,1,0:T(8,128)S(1)}, u32[]{:S(2)}, u32[]{:S(2)}) %all-to-all-start.1) | async-done | bytes 2097184 | tf_op jit(solution)/shard_map/all_to_all | solution.py:49
  243.5 1.5 multiply_bitcast_fusion
  245.1 1.9 copy.26
  247.0 141.5 %while.14 = (s32[]{:T(128)}, f32[512,1024]{0,1:T(8,128)S(1)}, s32[]{:T(128)}, s32[]{:T(128)}, f32[]{:T(128)}, /*index=5*/f32[]{:T(128)}, f32[]{:T(128)}, f32[]{:T(128)}, f32[]{:T(128)}) while((s32[]{:T(128)}, f32[512,1024]{0,1:T(8,128)S(1)}, s32[]{:T(128)}, s32[]{:T(128)}, f32[]{:T(128)}, /*index=5*/f32[]{:T(128)}, f32[]{:T(128)}, ...), condition=%wide.region_6.7_spmd.clone, body=%wide.region_1.6_spmd.clone.sunk | while | flops 13643786 | bytes 8453379 | solution.py:72
  247.0 0.6 multiply_reduce_fusion.2
  247.6 1.8 fusion.55
  249.5 1.0 fusion.57
  250.5 10.8 %all-reduce.2 = (f32[1024]{0:T(1024)S(1)}, f32[1024]{0:T(1024)S(1)}, f32[]{:T(128)}) all-reduce(f32[1024]{0:T(1024)S(1)} %bitcast.83, f32[1024]{0:T(1024)S(1)} %bitcast.84, f32[]{:T(128)} %get-tuple-element.117), channel_id=1, replica_groups=mesh['grp'=4,'inner'=8] {'grp'}, use_global_device_ids=true, to_apply=%region_5.5 | all-reduce | flops 2049 | bytes 16392 | tf_op jit(solution)/shard_map/while/body/eval_jaxpr/psum | solution.py:57
  261.3 0.7 dynamic_slice.24
  265.2 0.6 multiply_reduce_fusion.2
  265.8 1.8 fusion.55
  267.6 1.0 fusion.57
  268.7 9.9 %all-reduce.2 = (f32[1024]{0:T(1024)S(1)}, f32[1024]{0:T(1024)S(1)}, f32[]{:T(128)}) all-reduce(f32[1024]{0:T(1024)S(1)} %bitcast.83, f32[1024]{0:T(1024)S(1)} %bitcast.84, f32[]{:T(128)} %get-tuple-element.117), channel_id=1, replica_groups=mesh['grp'=4,'inner'=8] {'grp'}, use_global_device_ids=true, to_apply=%region_5.5 | all-reduce | flops 2049 | bytes 16392 | tf_op jit(solution)/shard_map/while/body/eval_jaxpr/psum | solution.py:57
  278.5 0.7 dynamic_slice.24
  282.4 0.6 multiply_reduce_fusion.2
  283.0 1.8 fusion.55
  284.9 1.0 fusion.57
  285.9 10.8 %all-reduce.2 = (f32[1024]{0:T(1024)S(1)}, f32[1024]{0:T(1024)S(1)}, f32[]{:T(128)}) all-reduce(f32[1024]{0:T(1024)S(1)} %bitcast.83, f32[1024]{0:T(1024)S(1)} %bitcast.84, f32[]{:T(128)} %get-tuple-element.117), channel_id=1, replica_groups=mesh['grp'=4,'inner'=8] {'grp'}, use_global_device_ids=true, to_apply=%region_5.5 | all-reduce | flops 2049 | bytes 16392 | tf_op jit(solution)/shard_map/while/body/eval_jaxpr/psum | solution.py:57
  296.7 0.7 dynamic_slice.24
  300.5 0.6 multiply_reduce_fusion.2
  301.1 1.8 fusion.55
  303.0 1.0 fusion.57
  304.0 9.9 %all-reduce.2 = (f32[1024]{0:T(1024)S(1)}, f32[1024]{0:T(1024)S(1)}, f32[]{:T(128)}) all-reduce(f32[1024]{0:T(1024)S(1)} %bitcast.83, f32[1024]{0:T(1024)S(1)} %bitcast.84, f32[]{:T(128)} %get-tuple-element.117), channel_id=1, replica_groups=mesh['grp'=4,'inner'=8] {'grp'}, use_global_device_ids=true, to_apply=%region_5.5 | all-reduce | flops 2049 | bytes 16392 | tf_op jit(solution)/shard_map/while/body/eval_jaxpr/psum | solution.py:57
  313.9 0.7 dynamic_slice.24
  317.8 0.6 multiply_reduce_fusion.2
  318.4 1.8 fusion.55
  320.2 1.0 fusion.57
  321.3 10.8 %all-reduce.2 = (f32[1024]{0:T(1024)S(1)}, f32[1024]{0:T(1024)S(1)}, f32[]{:T(128)}) all-reduce(f32[1024]{0:T(1024)S(1)} %bitcast.83, f32[1024]{0:T(1024)S(1)} %bitcast.84, f32[]{:T(128)} %get-tuple-element.117), channel_id=1, replica_groups=mesh['grp'=4,'inner'=8] {'grp'}, use_global_device_ids=true, to_apply=%region_5.5 | all-reduce | flops 2049 | bytes 16392 | tf_op jit(solution)/shard_map/while/body/eval_jaxpr/psum | solution.py:57
  332.1 0.7 dynamic_slice.24
  335.9 0.6 multiply_reduce_fusion.2
  336.5 1.8 fusion.55
  338.4 1.0 fusion.57
  339.4 9.9 %all-reduce.2 = (f32[1024]{0:T(1024)S(1)}, f32[1024]{0:T(1024)S(1)}, f32[]{:T(128)}) all-reduce(f32[1024]{0:T(1024)S(1)} %bitcast.83, f32[1024]{0:T(1024)S(1)} %bitcast.84, f32[]{:T(128)} %get-tuple-element.117), channel_id=1, replica_groups=mesh['grp'=4,'inner'=8] {'grp'}, use_global_device_ids=true, to_apply=%region_5.5 | all-reduce | flops 2049 | bytes 16392 | tf_op jit(solution)/shard_map/while/body/eval_jaxpr/psum | solution.py:57
  349.3 0.7 dynamic_slice.24
  353.2 0.6 multiply_reduce_fusion.2
  353.8 1.8 fusion.55
  355.6 1.0 fusion.57
  356.7 10.8 %all-reduce.2 = (f32[1024]{0:T(1024)S(1)}, f32[1024]{0:T(1024)S(1)}, f32[]{:T(128)}) all-reduce(f32[1024]{0:T(1024)S(1)} %bitcast.83, f32[1024]{0:T(1024)S(1)} %bitcast.84, f32[]{:T(128)} %get-tuple-element.117), channel_id=1, replica_groups=mesh['grp'=4,'inner'=8] {'grp'}, use_global_device_ids=true, to_apply=%region_5.5 | all-reduce | flops 2049 | bytes 16392 | tf_op jit(solution)/shard_map/while/body/eval_jaxpr/psum | solution.py:57
  367.4 0.7 dynamic_slice.24
  371.3 0.6 multiply_reduce_fusion.2
  371.9 1.8 fusion.55
  373.8 1.0 fusion.57
  374.8 9.9 %all-reduce.2 = (f32[1024]{0:T(1024)S(1)}, f32[1024]{0:T(1024)S(1)}, f32[]{:T(128)}) all-reduce(f32[1024]{0:T(1024)S(1)} %bitcast.83, f32[1024]{0:T(1024)S(1)} %bitcast.84, f32[]{:T(128)} %get-tuple-element.117), channel_id=1, replica_groups=mesh['grp'=4,'inner'=8] {'grp'}, use_global_device_ids=true, to_apply=%region_5.5 | all-reduce | flops 2049 | bytes 16392 | tf_op jit(solution)/shard_map/while/body/eval_jaxpr/psum | solution.py:57
  384.7 0.7 dynamic_slice.24
  388.5 1.8 copy.27
  (65 shorter events, 4.2 us)
Async XLA Ops:
  36.9 6.5 %copy-start = (s32[1,2048]{1,0:T(1,128)S(1)}, s32[1,2048]{1,0:T(1,128)}, u32[]{:S(2)}) copy-start(s32[1,2048]{1,0:T(1,128)} %param.7) | copy-start | bytes 24580
  36.9 54.7 %all-to-all-start = ((bf16[4,2,131072]{2,1,0:T(2,128)(2,1)}), bf16[4,2,131072]{2,1,0:T(2,128)(2,1)S(1)}, u32[]{:S(2)}, u32[]{:S(2)}) async-start(bf16[4,2,131072]{2,1,0:T(2,128)(2,1)} %reshape.93), calls=%async_computation | async-start | bytes 4194304 | tf_op jit(solution)/shard_map/all_to_all | solution.py:41
  43.4 148.5 %all-reduce.5.cloned.1.call-start = ((), (), s32[]{:S(2)}) async-start(), calls=%async_computation.2 | async-start | bytes 4194304 | tf_op jit(solution)/shard_map/psum | solution.py:48
  191.9 51.6 %all-to-all-start.1 = ((f32[4,512,256]{2,1,0:T(8,128)}), f32[4,512,256]{2,1,0:T(8,128)S(1)}, u32[]{:S(2)}, u32[]{:S(2)}) async-start(f32[4,512,256]{2,1,0:T(8,128)} %all-reduce.5.cloned.1.call-done), calls=%async_computation.1 | async-start | bytes 4194304 | tf_op jit(solution)/shard_map/all_to_all | solution.py:49
Sparse Core Ops, SparseCore 0:
  131.0 60.9 all-reduce.4
where the time goes:
time: 398 us; the launch traced here: 397 us
  waiting for transfers between devices  156 us (39%)
  blocking collectives  82.7 us (21%)
  local copies, waits for them, and re-layouts  56 us (14%)
  matrix products  28 us (7%)
  other arithmetic  27.4 us (7%)
  loops' own time  22.4 us (6%)
  between operations  13.5 us (3%)
  starting transfers between devices  11 us (3%)
    psum x8, blocking collectives, reflect(): lax.psum((jnp.sum(column * column), jnp.dot(column, current, precision=hi...  82.7 us
    psum x1, waiting for transfers between devices, on_device(): summed = lax.psum(partial_value, 'inner')  61.1 us
    all_to_all x1, waiting for transfers between devices, on_device(): lax.all_to_all(second_pass, 'grp', split_axis=2, concat_axis=1, tiled=True)  48.1 us
    all_to_all x1, waiting for transfers between devices, on_device(): lax.all_to_all(summed, 'grp', split_axis=0, concat_axis=1, tiled=True)  47.1 us
    another operation x1, loops' own time, on_device(): result = lax.fori_loop(0, COLS_DONE, reflect, sketch)  22.4 us
    gather x2, local copies, waits for them, and re-layouts, pick_rows(): return jnp.take(table_rows, chosen_rows, axis=0)  21.4 us
    dot_general x8, matrix products, reflect(): jnp.dot(column, current, precision=highest)  14.5 us
    unnamed x1, other arithmetic  12.8 us
  transfers between devices with their start and end apart: 3, of which 3 were waited for; matrix products, arithmetic and copies ran while one was open for 0% of the time, Pallas kernels for 0%

commit v1 on v0

--- a/solution.py
+++ b/solution.py
@@ -45,7 +45,8 @@
     mixed_rows = mixed_rows.reshape(block_count, 16 * 256, col_count)
     picked = jax.vmap(pick_rows)(mixed_rows, kept_rows)
     partial_value = jnp.sum(picked, axis=0)
-    summed = lax.psum(partial_value, "inner")
+    pieces = lax.all_gather(partial_value, "inner", axis=0, tiled=False)
+    summed = pieces.sum(axis=0)
     sketch = lax.all_to_all(summed, "grp", split_axis=0, concat_axis=1, tiled=True)
     sketch = sketch * (1.0 / (64.0 * math.sqrt(keep_count)))
     row_base = lax.axis_index("grp") * owned_rows

time: 398 us -> 435 us (1.093)
  waiting for transfers between devices: 156 us -> 186 us
  other arithmetic: 27.4 us -> 35.9 us
    all_gather x0 -> x1, waiting for transfers between devices: none -> 89 us  [on_device(): pieces = lax.all_gather(partial_value, 'inner', axis=0, tiled=False)]
    psum x1 -> x0, waiting for transfers between devices: 61.1 us -> none  [on_device(): summed = lax.psum(partial_value, 'inner')]
    reduce_sum x0 -> x1, other arithmetic: none -> 8.45 us  [on_device(): summed = pieces.sum(axis=0)]
where the time goes in v1:
time: 435 us; the launch traced here: 434 us
  waiting for transfers between devices  186 us (43%)
  blocking collectives  82.7 us (19%)
  local copies, waits for them, and re-layouts  55.6 us (13%)
  other arithmetic  35.9 us (8%)
  matrix products  28 us (6%)
  loops' own time  21.5 us (5%)
  between operations  13.5 us (3%)
  starting transfers between devices  11.1 us (3%)
    all_gather x1, waiting for transfers between devices, on_device(): pieces = lax.all_gather(partial_value, 'inner', axis=0, tiled=False)  89 us
    psum x8, blocking collectives, reflect(): lax.psum((jnp.sum(column * column), jnp.dot(column, current, precision=hi...  82.7 us
    all_to_all x1, waiting for transfers between devices, on_device(): lax.all_to_all(summed, 'grp', split_axis=0, concat_axis=1, tiled=True)  48.6 us
    all_to_all x1, waiting for transfers between devices, on_device(): lax.all_to_all(second_pass, 'grp', split_axis=2, concat_axis=1, tiled=True)  48.1 us
    another operation x1, loops' own time, on_device(): result = lax.fori_loop(0, COLS_DONE, reflect, sketch)  21.5 us
    gather x2, local copies, waits for them, and re-layouts, pick_rows(): return jnp.take(table_rows, chosen_rows, axis=0)  21.4 us
    dot_general x8, matrix products, reflect(): jnp.dot(column, current, precision=highest)  14.5 us
    unnamed x1, other arithmetic  12.8 us
  transfers between devices with their start and end apart: 3, of which 3 were waited for; matrix products, arithmetic and copies ran while one was open for 0% of the time, Pallas kernels for 0%

profile of v1, /device:TPU:0, one launch (start us, length us, event | category | flops | bytes accessed | tf_op | source)
XLA Modules:
  0.0 433.9 jit_solution(13699200696126563588)
XLA Ops:
  6.5 0.7 subtract_convert_fusion.4
  7.2 2.5 multiply_convert_fusion
  9.7 0.7 convolution_convert_fusion
  10.4 1.5 convert_bitcast_fusion
  11.9 1.2 copy.26
  13.1 7.7 %copy.27 = bf16[1,1024,1024]{1,0,2:T(2,128)(2,1)} copy(bf16[1,1024,1024]{2,1,0:T(8,128)(2,1)S(1)} %bitcast.79) | data formatting | bytes 4194304 | tf_op jit(solution)/shard_map/reshape | solution.py:40
  21.4 12.8 %reduce.2 = bf16[1024,1024]{1,0:T(8,128)(2,1)S(1)} reduce(bf16[1024,1,1024]{2,1,0:T(2,128)(2,1)} %bitcast.77, bf16[]{:T(256)} %broadcast.129), dimensions={1}, to_apply=%bitcast.45.reduce_sub_computation | reduce | bytes 4194306
  34.2 2.8 reshape.118
  36.9 6.5 %all-to-all-start = ((bf16[4,2,131072]{2,1,0:T(2,128)(2,1)}), bf16[4,2,131072]{2,1,0:T(2,128)(2,1)S(1)}, u32[]{:S(2)}, u32[]{:S(2)}) async-start(bf16[4,2,131072]{2,1,0:T(2,128)(2,1)} %reshape.118), calls=%async_computation | async-start | bytes 4194304 | tf_op jit(solution)/shard_map/all_to_all | solution.py:41
  43.5 48.1 %all-to-all-done = bf16[4,2,131072]{2,1,0:T(2,128)(2,1)S(1)} async-done(((bf16[4,2,131072]{2,1,0:T(2,128)(2,1)}), bf16[4,2,131072]{2,1,0:T(2,128)(2,1)S(1)}, u32[]{:S(2)}, u32[]{:S(2)}) %all-to-all-start) | async-done | bytes 2097184 | tf_op jit(solution)/shard_map/all_to_all | solution.py:41
  91.6 3.4 reshape.119
  94.9 3.0 copy.34
  97.9 2.6 copy.28
  100.5 2.9 convolution_bitcast_fusion
  103.4 4.4 %copy.30 = f32[1,16,256,256]{3,2,1,0:T(8,128)} copy(f32[1,16,256,256]{3,1,2,0:T(8,128)S(1)} %convolution_bitcast_fusion) | data formatting | bytes 8388608 | tf_op jit(solution)/shard_map/ha,nakd->nhkd/transpose | solution.py:44
  107.8 21.4 %gather_fusion = f32[2048,256]{1,0:T(8,128)S(1)} fusion(f32[1,4096,256]{2,1,0:T(8,128)} %bitcast.76, s32[2048]{0:T(1024)S(1)} %bitcast.75), kind=kCustom, calls=%fused_computation | custom fusion | bytes 4210688 | tf_op jit(solution)/shard_map/vmap(jit(_take))/gather | solution.py:20
  129.2 1.7 bitcast_select_fusion
  130.8 89.0 %all-gather.2.cloned.1.call-done = f32[8,2048,256]{2,1,0:T(8,128)} async-done(((f32[1,2048,256]{2,1,0:T(8,128)}), f32[8,2048,256]{2,1,0:T(8,128)}) %all-gather.2.cloned.1.call-update) | async-done | bytes 16777232 | tf_op jit(solution)/shard_map/all_gather | solution.py:48
  219.9 8.5 %reduce_sum.26 = f32[2048,256]{1,0:T(8,128)} reduce(f32[8,2048,256]{2,1,0:T(8,128)} %all-gather.2.cloned.1.call-done, f32[]{:T(128)} %constant.93.clone.1), dimensions={0}, to_apply=%region_0.1 | reduce | flops 3670016 | bytes 18874372 | tf_op jit(solution)/shard_map/reduce_sum | solution.py:49
  228.3 4.6 %all-to-all-start.1 = ((f32[4,512,256]{2,1,0:T(8,128)}), f32[4,512,256]{2,1,0:T(8,128)S(1)}, u32[]{:S(2)}, u32[]{:S(2)}) async-start(f32[4,512,256]{2,1,0:T(8,128)} %bitcast.84), calls=%async_computation.1 | async-start | bytes 4194304 | tf_op jit(solution)/shard_map/all_to_all | solution.py:50
  232.9 48.6 %all-to-all-done.1 = f32[4,512,256]{2,1,0:T(8,128)S(1)} async-done(((f32[4,512,256]{2,1,0:T(8,128)}), f32[4,512,256]{2,1,0:T(8,128)S(1)}, u32[]{:S(2)}, u32[]{:S(2)}) %all-to-all-start.1) | async-done | bytes 2097184 | tf_op jit(solution)/shard_map/all_to_all | solution.py:50
  281.5 1.5 multiply_bitcast_fusion
  283.1 1.9 copy.31
  285.0 140.2 %while.14 = (s32[]{:T(128)}, f32[512,1024]{0,1:T(8,128)S(1)}, s32[]{:T(128)}, s32[]{:T(128)}, f32[]{:T(128)}, /*index=5*/f32[]{:T(128)}, f32[]{:T(128)}, f32[]{:T(128)}, f32[]{:T(128)}) while((s32[]{:T(128)}, f32[512,1024]{0,1:T(8,128)S(1)}, s32[]{:T(128)}, s32[]{:T(128)}, f32[]{:T(128)}, /*index=5*/f32[]{:T(128)}, f32[]{:T(128)}, ...), condition=%wide.region_6.7_spmd.clone, body=%wide.region_1.6_spmd.clone.sunk | while | flops 13643786 | bytes 8453379 | solution.py:73
  285.0 0.6 multiply_reduce_fusion.2
  285.6 1.8 fusion.55
  287.5 1.0 fusion.57
  288.5 10.8 %all-reduce.2 = (f32[1024]{0:T(1024)S(1)}, f32[1024]{0:T(1024)S(1)}, f32[]{:T(128)}) all-reduce(f32[1024]{0:T(1024)S(1)} %bitcast.85, f32[1024]{0:T(1024)S(1)} %bitcast.86, f32[]{:T(128)} %get-tuple-element.117), channel_id=1, replica_groups=mesh['grp'=4,'inner'=8] {'grp'}, use_global_device_ids=true, to_apply=%region_5.5 | all-reduce | flops 2049 | bytes 16392 | tf_op jit(solution)/shard_map/while/body/eval_jaxpr/psum | solution.py:58
  299.3 0.6 dynamic_slice.24
  303.0 0.6 multiply_reduce_fusion.2
  303.6 1.8 fusion.55
  305.4 1.0 fusion.57
  306.5 9.9 %all-reduce.2 = (f32[1024]{0:T(1024)S(1)}, f32[1024]{0:T(1024)S(1)}, f32[]{:T(128)}) all-reduce(f32[1024]{0:T(1024)S(1)} %bitcast.85, f32[1024]{0:T(1024)S(1)} %bitcast.86, f32[]{:T(128)} %get-tuple-element.117), channel_id=1, replica_groups=mesh['grp'=4,'inner'=8] {'grp'}, use_global_device_ids=true, to_apply=%region_5.5 | all-reduce | flops 2049 | bytes 16392 | tf_op jit(solution)/shard_map/while/body/eval_jaxpr/psum | solution.py:58
  316.4 0.6 dynamic_slice.24
  320.1 0.6 multiply_reduce_fusion.2
  320.7 1.8 fusion.55
  322.5 1.0 fusion.57
  323.6 10.8 %all-reduce.2 = (f32[1024]{0:T(1024)S(1)}, f32[1024]{0:T(1024)S(1)}, f32[]{:T(128)}) all-reduce(f32[1024]{0:T(1024)S(1)} %bitcast.85, f32[1024]{0:T(1024)S(1)} %bitcast.86, f32[]{:T(128)} %get-tuple-element.117), channel_id=1, replica_groups=mesh['grp'=4,'inner'=8] {'grp'}, use_global_device_ids=true, to_apply=%region_5.5 | all-reduce | flops 2049 | bytes 16392 | tf_op jit(solution)/shard_map/while/body/eval_jaxpr/psum | solution.py:58
  334.3 0.6 dynamic_slice.24
  338.6 1.8 fusion.55
  340.5 1.0 fusion.57
  341.5 9.9 %all-reduce.2 = (f32[1024]{0:T(1024)S(1)}, f32[1024]{0:T(1024)S(1)}, f32[]{:T(128)}) all-reduce(f32[1024]{0:T(1024)S(1)} %bitcast.85, f32[1024]{0:T(1024)S(1)} %bitcast.86, f32[]{:T(128)} %get-tuple-element.117), channel_id=1, replica_groups=mesh['grp'=4,'inner'=8] {'grp'}, use_global_device_ids=true, to_apply=%region_5.5 | all-reduce | flops 2049 | bytes 16392 | tf_op jit(solution)/shard_map/while/body/eval_jaxpr/psum | solution.py:58
  351.4 0.6 dynamic_slice.24
  355.1 0.6 multiply_reduce_fusion.2
  355.7 1.8 fusion.55
  357.6 1.0 fusion.57
  358.6 10.8 %all-reduce.2 = (f32[1024]{0:T(1024)S(1)}, f32[1024]{0:T(1024)S(1)}, f32[]{:T(128)}) all-reduce(f32[1024]{0:T(1024)S(1)} %bitcast.85, f32[1024]{0:T(1024)S(1)} %bitcast.86, f32[]{:T(128)} %get-tuple-element.117), channel_id=1, replica_groups=mesh['grp'=4,'inner'=8] {'grp'}, use_global_device_ids=true, to_apply=%region_5.5 | all-reduce | flops 2049 | bytes 16392 | tf_op jit(solution)/shard_map/while/body/eval_jaxpr/psum | solution.py:58
  369.4 0.6 dynamic_slice.24
  373.1 0.6 multiply_reduce_fusion.2
  373.7 1.8 fusion.55
  375.5 1.0 fusion.57
  376.6 9.9 %all-reduce.2 = (f32[1024]{0:T(1024)S(1)}, f32[1024]{0:T(1024)S(1)}, f32[]{:T(128)}) all-reduce(f32[1024]{0:T(1024)S(1)} %bitcast.85, f32[1024]{0:T(1024)S(1)} %bitcast.86, f32[]{:T(128)} %get-tuple-element.117), channel_id=1, replica_groups=mesh['grp'=4,'inner'=8] {'grp'}, use_global_device_ids=true, to_apply=%region_5.5 | all-reduce | flops 2049 | bytes 16392 | tf_op jit(solution)/shard_map/while/body/eval_jaxpr/psum | solution.py:58
  386.5 0.6 dynamic_slice.24
  390.2 0.6 multiply_reduce_fusion.2
  390.8 1.8 fusion.55
  392.6 1.0 fusion.57
  393.7 10.8 %all-reduce.2 = (f32[1024]{0:T(1024)S(1)}, f32[1024]{0:T(1024)S(1)}, f32[]{:T(128)}) all-reduce(f32[1024]{0:T(1024)S(1)} %bitcast.85, f32[1024]{0:T(1024)S(1)} %bitcast.86, f32[]{:T(128)} %get-tuple-element.117), channel_id=1, replica_groups=mesh['grp'=4,'inner'=8] {'grp'}, use_global_device_ids=true, to_apply=%region_5.5 | all-reduce | flops 2049 | bytes 16392 | tf_op jit(solution)/shard_map/while/body/eval_jaxpr/psum | solution.py:58
  404.4 0.6 dynamic_slice.24
  408.1 0.6 multiply_reduce_fusion.2
  408.7 1.8 fusion.55
  410.6 1.0 fusion.57
  411.6 9.9 %all-reduce.2 = (f32[1024]{0:T(1024)S(1)}, f32[1024]{0:T(1024)S(1)}, f32[]{:T(128)}) all-reduce(f32[1024]{0:T(1024)S(1)} %bitcast.85, f32[1024]{0:T(1024)S(1)} %bitcast.86, f32[]{:T(128)} %get-tuple-element.117), channel_id=1, replica_groups=mesh['grp'=4,'inner'=8] {'grp'}, use_global_device_ids=true, to_apply=%region_5.5 | all-reduce | flops 2049 | bytes 16392 | tf_op jit(solution)/shard_map/while/body/eval_jaxpr/psum | solution.py:58
  421.5 0.6 dynamic_slice.24
  425.2 1.8 copy.32
  (66 shorter events, 4.8 us)
Async XLA Ops:
  36.9 6.5 %copy-start = (s32[1,2048]{1,0:T(1,128)S(1)}, s32[1,2048]{1,0:T(1,128)}, u32[]{:S(2)}) copy-start(s32[1,2048]{1,0:T(1,128)} %param.7) | copy-start | bytes 24580
  36.9 54.7 %all-to-all-start = ((bf16[4,2,131072]{2,1,0:T(2,128)(2,1)}), bf16[4,2,131072]{2,1,0:T(2,128)(2,1)S(1)}, u32[]{:S(2)}, u32[]{:S(2)}) async-start(bf16[4,2,131072]{2,1,0:T(2,128)(2,1)} %reshape.118), calls=%async_computation | async-start | bytes 4194304 | tf_op jit(solution)/shard_map/all_to_all | solution.py:41
  43.4 176.5 %all-gather.2.cloned.1.call-start = ((), (), s32[]{:S(2)}) async-start(), calls=%async_computation.2 | async-start | bytes 18874368 | tf_op jit(solution)/shard_map/all_gather | solution.py:48
  228.3 53.2 %all-to-all-start.1 = ((f32[4,512,256]{2,1,0:T(8,128)}), f32[4,512,256]{2,1,0:T(8,128)S(1)}, u32[]{:S(2)}, u32[]{:S(2)}) async-start(f32[4,512,256]{2,1,0:T(8,128)} %bitcast.84), calls=%async_computation.1 | async-start | bytes 4194304 | tf_op jit(solution)/shard_map/all_to_all | solution.py:50
Sparse Core Ops, SparseCore 0:
  131.0 88.8 all-gather.1
